TPU v7x, 32 devices: a whole 2x2x4 slice. The times are simulated.
32 devices in a mesh: node: 8 (over y, x, core), local: 4 (over z).
Axes of the slice: x: 2, y: 2, z: 4, core: 2. Of those that a mesh axis runs over, the one named last changes fastest.
Arguments:
- tokens: bfloat16 [4096, 4096], P(('node', 'local')), may hold values from -6 to 6
- grad_out: bfloat16 [4096, 4096], P(('node', 'local')), may hold values from -6 to 6
- router_logits: float32 [4096, 128], P(('node', 'local')), may hold values from -20 to 280
- group_id: int32 [4096], P(('node', 'local')), may hold values from 0 to 15, as said below
- expert_ids: int32 [4096, 2], P(('node', 'local')), may hold values from 0 to 7, as said below
- w_gate: bfloat16 [8, 4096, 1536], P('node', None, 'local'), may hold values from -0.09375 to 0.09375
- w_up: bfloat16 [8, 4096, 1536], P('node', None, 'local'), may hold values from -0.09375 to 0.09375
- w_down: bfloat16 [8, 1536, 4096], P('node', 'local'), may hold values from -0.15625 to 0.15625
Outputs:
- mixed: bfloat16 [4096, 4096], P(('node', 'local'))
- d_tokens: bfloat16 [4096, 4096], P(('node', 'local'))
- d_logits: float32 [4096, 128], P(('node', 'local'))
- grad_gate: bfloat16 [8, 4096, 1536], P('node', None, 'local')
- grad_up: bfloat16 [8, 4096, 1536], P('node', None, 'local')
- grad_down: bfloat16 [8, 1536, 4096], P('node', 'local')
Inputs may be any that keep to these rules, and one draw needn't show every extreme that they name: `group_id`: A token is computed here when its group is below 1. Among the tokens of one device no expert of those groups is named by more than 6 tokens, and one such expert is named by exactly 6 tokens of every device. `expert_ids`: the two numbers of a token differ; both name experts of the token's group.
All inputs are finite; a program needn't handle non-finite values.
Results may differ from a plain program's by a relative error of at most 0.0065.
Values may be sent and summed in bfloat16 or wider, within the bound.
A program may use at most 192 MiB of HBM per device.

v0:
```python
import jax
import jax.numpy as jnp
from jax import lax
from jax.sharding import PartitionSpec as P

GSIZE = 8
CAP = 6


def gate_weights(logits, group_ids, chosen, inside):
    probabilities = jax.nn.softmax(logits, axis=-1)
    columns = jnp.arange(logits.shape[1], dtype=jnp.int32)
    member = ((columns // GSIZE)[None, :] == group_ids[:, None]).astype(logits.dtype)
    group_mass = jnp.sum(probabilities * member, axis=1)
    picked = jnp.sum(
        jnp.where(chosen[:, :, None] == columns[None, None, :], logits[:, None, :], 0.0), axis=2
    )
    pair_share = jax.nn.softmax(picked, axis=-1)
    return jnp.where(inside[:, None], group_mass[:, None] * pair_share, 0.0)


def spread(buffer):
    arrived = lax.all_to_all(buffer, "node", split_axis=0, concat_axis=2, tiled=True)
    arrived = lax.all_gather(arrived, "local", axis=2, tiled=True)
    return arrived[0]


def collect(partial_sums):
    summed = lax.psum_scatter(partial_sums[None], "local", scatter_dimension=2, tiled=True)
    result = lax.all_to_all(
        summed.astype(jnp.bfloat16), "node", split_axis=2, concat_axis=0, tiled=True
    )
    return result.reshape(-1, result.shape[-1])


def body(tokens, grad_out, router_logits, group_id, expert_ids, w_gate, w_up, w_down):
    owned_count = w_gate.shape[0]
    node_count = lax.axis_size("node")
    expert_total = owned_count * node_count
    window_groups = expert_total // GSIZE
    model_width = tokens.shape[1]
    inside = group_id < window_groups
    chosen = group_id[:, None] * GSIZE + expert_ids
    target = jnp.where(inside[:, None], chosen, expert_total)
    expert_range = jnp.arange(expert_total, dtype=jnp.int32)
    onehot = (target[:, :, None] == expert_range[None, None, :]).astype(jnp.int32)
    per_token = jnp.sum(onehot, axis=1)
    earlier = jnp.cumsum(per_token, axis=0) - per_token
    slot_rank = jnp.sum(onehot * earlier[:, None, :], axis=2)
    slot_index = jnp.where(inside[:, None], target * CAP + slot_rank, -1)
    slot_range = jnp.arange(expert_total * CAP, dtype=jnp.int32)
    first_pick = (slot_range[:, None] == slot_index[None, :, 0]).astype(jnp.bfloat16)
    second_pick = (slot_range[:, None] == slot_index[None, :, 1]).astype(jnp.bfloat16)
    mix_weights, pull_back = jax.vjp(
        lambda values: gate_weights(values, group_id, chosen, inside), router_logits
    )
    grad_f32 = grad_out.astype(jnp.float32)
    first_grad = (mix_weights[:, 0:1] * grad_f32).astype(jnp.bfloat16)
    second_grad = (mix_weights[:, 1:2] * grad_f32).astype(jnp.bfloat16)
    send_rows = (
        jnp.dot(first_pick, tokens, preferred_element_type=jnp.float32)
        + jnp.dot(second_pick, tokens, preferred_element_type=jnp.float32)
    ).astype(jnp.bfloat16)
    send_grads = (
        jnp.dot(first_pick, first_grad, preferred_element_type=jnp.float32)
        + jnp.dot(second_pick, second_grad, preferred_element_type=jnp.float32)
    ).astype(jnp.bfloat16)
    buffer_shape = (node_count, owned_count, CAP, model_width)
    rows_in = spread(send_rows.reshape(buffer_shape))
    gate_pre = jnp.einsum("erd,edf->erf", rows_in, w_gate, preferred_element_type=jnp.float32)
    up_pre = jnp.einsum("erd,edf->erf", rows_in, w_up, preferred_element_type=jnp.float32)
    sigmoid_gate = jax.nn.sigmoid(gate_pre)
    activated = gate_pre * sigmoid_gate
    hidden = (activated * up_pre).astype(jnp.bfloat16)
    partial_out = jnp.einsum("erf,efd->erd", hidden, w_down, preferred_element_type=jnp.float32)
    out_flat = collect(partial_out)
    grads_in = spread(send_grads.reshape(buffer_shape))
    grad_hidden = jnp.einsum("erd,efd->erf", grads_in, w_down, preferred_element_type=jnp.float32)
    grad_gate_pre = (
        grad_hidden * up_pre * sigmoid_gate * (1.0 + gate_pre * (1.0 - sigmoid_gate))
    ).astype(jnp.bfloat16)
    grad_up_pre = (grad_hidden * activated).astype(jnp.bfloat16)
    partial_in = jnp.einsum(
        "erf,edf->erd", grad_gate_pre, w_gate, preferred_element_type=jnp.float32
    ) + jnp.einsum("erf,edf->erd", grad_up_pre, w_up, preferred_element_type=jnp.float32)
    back_flat = collect(partial_in)
    grad_gate = jnp.einsum(
        "erd,erf->edf", rows_in, grad_gate_pre, preferred_element_type=jnp.float32
    ).astype(jnp.bfloat16)
    grad_up = jnp.einsum(
        "erd,erf->edf", rows_in, grad_up_pre, preferred_element_type=jnp.float32
    ).astype(jnp.bfloat16)
    grad_down = jnp.einsum(
        "erf,erd->efd", hidden, grads_in, preferred_element_type=jnp.float32
    ).astype(jnp.bfloat16)
    first_out = jnp.einsum("st,sd->td", first_pick, out_flat, preferred_element_type=jnp.float32)
    second_out = jnp.einsum("st,sd->td", second_pick, out_flat, preferred_element_type=jnp.float32)
    first_back = jnp.einsum("st,sd->td", first_pick, back_flat, preferred_element_type=jnp.float32)
    second_back = jnp.einsum(
        "st,sd->td", second_pick, back_flat, preferred_element_type=jnp.float32
    )
    mixed = (mix_weights[:, 0:1] * first_out + mix_weights[:, 1:2] * second_out).astype(
        jnp.bfloat16
    )
    d_tokens = (first_back + second_back).astype(jnp.bfloat16)
    scores = jnp.stack(
        [jnp.sum(grad_f32 * first_out, axis=1), jnp.sum(grad_f32 * second_out, axis=1)], axis=1
    )
    d_logits = pull_back(scores)[0]
    return (mixed, d_tokens, d_logits, grad_gate, grad_up, grad_down)


def solution(mesh):
    return jax.shard_map(
        body,
        mesh=mesh,
        in_specs=(
            P(("node", "local"), None),
            P(("node", "local"), None),
            P(("node", "local"), None),
            P(("node", "local")),
            P(("node", "local"), None),
            P("node", None, "local"),
            P("node", None, "local"),
            P("node", "local", None),
        ),
        out_specs=(
            P(("node", "local"), None),
            P(("node", "local"), None),
            P(("node", "local"), None),
            P("node", None, "local"),
            P("node", None, "local"),
            P("node", "local", None),
        ),
        check_vma=False,
    )
```

profile of v0, /device:TPU:0, one launch (start us, length us, event | category | flops | bytes accessed | tf_op | source)
XLA Modules:
  0.0 320.4 jit_solution(9817088539204725255)
XLA Ops:
  7.2 0.8 broadcast_compare_fusion
  8.0 0.8 broadcast_multiply_fusion
  8.8 0.7 broadcast_select_fusion
  9.5 0.1 copy.34
  9.6 0.2 reduce_window_sum.11
  9.9 1.6 fusion.51
  11.5 0.3 fusion.5
  11.8 0.9 reshape.170
  12.7 15.0 %all_to_all.42 = bf16[8,1,6,4096]{3,2,1,0:T(8,128)(2,1)} all-to-all(bf16[8,1,6,4096]{3,2,1,0:T(8,128)(2,1)} %bitcast.93), channel_id=1, replica_groups=mesh['node'=8,'local'=4] {'node'}, dimensions={0} | all-to-all | bytes 786432 | tf_op jit(solution)/shard_map/all_to_all | solution.py:23
  27.7 1.9 all_to_all.13
  29.7 36.8 %all-gather.3.cloned.1.call-done = bf16[1,1,192,4096]{3,2,1,0:T(8,128)(2,1)} async-done(((bf16[1,1,48,4096]{3,2,1,0:T(8,128)(2,1)}), bf16[1,1,192,4096]{3,2,1,0:T(8,128)(2,1)}) %all-gather.3.cloned.1.call-update) | async-done | bytes 1572880 | tf_op jit(solution)/shard_map/all_gather | solution.py:24
  66.5 3.5 %fusion.15 = f32[192,384]{1,0:T(8,128)S(1)} fusion(bf16[1,4096,384]{2,1,0:T(8,128)(2,1)} %param.13, bf16[1,1,192,4096]{3,2,1,0:T(8,128)(2,1)} %all-gather.3.cloned.1.call-done), kind=kOutput, calls=%fused_computation.27 | convolution fusion | flops 603979776 | bytes 5013504 | tf_op jit(solution)/shard_map/erd,edf->erf/dot_general | solution.py:70
  70.0 0.3 copy-done.10
  70.3 1.7 multiply_convert_fusion.2
  72.0 0.6 copy-done.13
  72.6 2.7 convolution_bitcast_fusion
  75.3 0.8 copy-done.9
  76.1 0.2 select_reduce_fusion.1
  76.4 0.5 multiply_divide_fusion.1
  76.9 57.9 %reduce-scatter.3.cloned.1.call-done = f32[1,1,48,4096]{3,2,1,0:T(8,128)} async-done(((f32[1,1,192,4096]{3,2,1,0:T(8,128)}), f32[1,1,48,4096]{3,2,1,0:T(8,128)}) %reduce-scatter.3.cloned.1.call-update) | async-done | bytes 786448 | tf_op jit(solution)/shard_map/reduce_scatter | solution.py:29
  134.8 1.2 convert_element_type.66
  135.9 1.7 copy.64
  137.7 0.6 broadcast.90
  138.3 4.9 %reduce = bf16[48,4096]{1,0:T(8,128)(2,1)} reduce(bf16[48,1,1,4096]{3,2,1,0:T(2,128)(2,1)} %bitcast.87, bf16[]{:T(256)} %broadcast.90), dimensions={1,2}, to_apply=%bitcast.86.reduce_sub_computation | reduce | bytes 786434
  143.1 2.1 reshape.179
  145.2 4.1 %all-to-all-start.1 = ((bf16[8,2,12288]{2,1,0:T(2,128)(2,1)}), bf16[8,2,12288]{2,1,0:T(2,128)(2,1)}, u32[]{:S(2)}, u32[]{:S(2)}) async-start(bf16[8,2,12288]{2,1,0:T(2,128)(2,1)} %reshape.179), calls=%async_computation.2 | async-start | bytes 786432 | tf_op jit(solution)/shard_map/all_to_all | solution.py:30
  149.3 0.5 and_select_fusion
  149.9 0.1 reduce_max.18
  150.0 0.2 fusion.50
  150.2 0.5 multiply_divide_fusion
  150.7 6.9 %all-to-all-done.1 = bf16[8,2,12288]{2,1,0:T(2,128)(2,1)} async-done(((bf16[8,2,12288]{2,1,0:T(2,128)(2,1)}), bf16[8,2,12288]{2,1,0:T(2,128)(2,1)}, u32[]{:S(2)}, u32[]{:S(2)}) %all-to-all-start.1) | async-done | bytes 393248 | tf_op jit(solution)/shard_map/all_to_all | solution.py:30
  157.6 3.4 %reshape.180 = bf16[48,1,1,4096]{3,2,1,0:T(2,128)(2,1)} reshape(bf16[8,2,12288]{2,1,0:T(2,128)(2,1)} %all-to-all-done.1) | data formatting | bytes 786432
  161.0 2.0 fusion.35
  163.1 2.2 fusion.19
  165.3 0.7 fusion.49
  166.1 1.2 add_multiply_fusion
  167.3 0.4 fusion.28
  167.7 1.2 fusion.6
  168.9 1.9 reshape.176
  170.8 13.8 %all_to_all.43 = bf16[8,1,6,4096]{3,2,1,0:T(8,128)(2,1)} all-to-all(bf16[8,1,6,4096]{3,2,1,0:T(8,128)(2,1)} %bitcast.94), channel_id=1, replica_groups=mesh['node'=8,'local'=4] {'node'}, dimensions={0} | all-to-all | bytes 786432 | tf_op jit(solution)/shard_map/all_to_all | solution.py:23
  184.6 1.9 all_to_all.16
  186.6 0.2 reduce-scatter.5.cloned.1.call-start
  186.8 35.0 %all-gather.5.cloned.1.call-done = bf16[1,1,192,4096]{3,2,1,0:T(8,128)(2,1)} async-done(((bf16[1,1,48,4096]{3,2,1,0:T(8,128)(2,1)}), bf16[1,1,192,4096]{3,2,1,0:T(8,128)(2,1)}) %all-gather.5.cloned.1.call-update) | async-done | bytes 1572880 | tf_op jit(solution)/shard_map/all_gather | solution.py:24
  221.8 2.8 multiply_convert_fusion
  224.7 1.2 fusion.13
  225.9 0.7 copy-done.7
  226.6 2.9 fusion
  229.6 0.6 copy-done.24
  230.2 0.1 select_reduce_fusion
  230.4 0.8 fusion.46
  231.2 3.8 %add_convert_fusion = bf16[128,4096]{1,0:T(8,128)(2,1)} fusion(f32[128,4096]{1,0:T(8,128)} %copy-done.1, f32[128,4096]{1,0:T(8,128)} %get-tuple-element.24, f32[128]{0:T(128)S(1)} %get-tuple-element.19, f32[128]{0:T(128)S(1)} %get-tuple-element.18), kind=kLoop, calls=%fused_computation.33 | loop fusion | flops 2097152 | bytes 5243904 | tf_op jit(solution)/shard_map/convert_element_type | solution.py:102
  234.9 3.0 fusion.1
  237.9 51.1 %reduce-scatter.5.cloned.1.call-done = f32[1,1,48,4096]{3,2,1,0:T(8,128)} async-done(((f32[1,1,192,4096]{3,2,1,0:T(8,128)}), f32[1,1,48,4096]{3,2,1,0:T(8,128)}) %reduce-scatter.5.cloned.1.call-update) | async-done | bytes 786448 | tf_op jit(solution)/shard_map/reduce_scatter | solution.py:29
  289.0 1.2 convert_element_type.74
  290.2 1.7 copy.63
  291.9 4.1 %reduce.1 = bf16[48,4096]{1,0:T(8,128)(2,1)S(1)} reduce(bf16[48,1,1,4096]{3,2,1,0:T(2,128)(2,1)} %bitcast.88, bf16[]{:T(256)} %broadcast.90), dimensions={1,2}, to_apply=%bitcast.85.reduce_sub_computation | reduce | bytes 786434
  296.0 1.1 reshape.181
  297.1 3.7 %all-to-all-start.3 = ((bf16[8,2,12288]{2,1,0:T(2,128)(2,1)}), bf16[8,2,12288]{2,1,0:T(2,128)(2,1)S(1)}, u32[]{:S(2)}, u32[]{:S(2)}) async-start(bf16[8,2,12288]{2,1,0:T(2,128)(2,1)} %reshape.181), calls=%async_computation.5 | async-start | bytes 786432 | tf_op jit(solution)/shard_map/all_to_all | solution.py:30
  300.8 4.3 %fusion.3 = bf16[1,384,4096]{2,1,0:T(8,128)(2,1)} fusion(bf16[192,384]{1,0:T(8,128)(2,1)} %copy-done.13, bf16[1,1,192,4096]{3,2,1,0:T(8,128)(2,1)} %all-gather.5.cloned.1.call-done), kind=kOutput, calls=%fused_computation.7 | convolution fusion | flops 605552640 | bytes 4866048 | tf_op jit(solution)/shard_map/erf,erd->efd/dot_general | solution.py:93
  305.1 3.0 fusion.2
  308.1 1.0 all-to-all-done.3
  309.1 1.1 reshape.182
  310.2 1.9 fusion.33
  312.1 1.7 fusion.4
  (69 shorter events, 0.6 us)
Async XLA Ops:
  7.2 65.5 %copy-start = (bf16[1,384,4096]{2,1,0:T(8,128)(2,1)S(1)}, bf16[1,384,4096]{2,1,0:T(8,128)(2,1)}, u32[]{:S(2)}) copy-start(bf16[1,384,4096]{2,1,0:T(8,128)(2,1)} %param.15) | copy-start | bytes 9437188
  7.2 59.3 %all-gather.3.cloned.1.call-start = ((), (), s32[]{:S(2)}) async-start(), calls=%async_computation.6 | async-start | bytes 1966080 | tf_op jit(solution)/shard_map/all_gather | solution.py:24
  9.8 1.7 copy-start.4
  29.7 105.1 %reduce-scatter.3.cloned.1.call-start = ((), (), s32[]{:S(2)}) async-start(), calls=%async_computation.7 | async-start | bytes 3932160 | tf_op jit(solution)/shard_map/reduce_scatter | solution.py:29
  66.5 3.5 %copy-start.6 = (bf16[1,4096,384]{2,1,0:T(8,128)(2,1)S(1)}, bf16[1,4096,384]{2,1,0:T(8,128)(2,1)}, u32[]{:S(2)}) copy-start(bf16[1,4096,384]{2,1,0:T(8,128)(2,1)} %param.14) | copy-start | bytes 9437188
  66.5 3.8 %copy-start.10 = (bf16[1,1,192,4096]{3,2,1,0:T(8,128)(2,1)S(1)}, bf16[1,1,192,4096]{3,2,1,0:T(8,128)(2,1)}, u32[]{:S(2)}) copy-start(bf16[1,1,192,4096]{3,2,1,0:T(8,128)(2,1)} %all-gather.3.cloned.1.call-done) | copy-start | bytes 4718596
  72.0 0.6 copy-start.13
  75.3 0.8 copy-start.9
  76.4 88.9 %copy-start.18 = (f32[128]{0:T(128)}, f32[128]{0:T(128)S(1)}, u32[]{:S(2)}) copy-start(f32[128]{0:T(128)S(1)} %fusion.60) | copy-start | bytes 1540
  145.2 12.4 %all-to-all-start.1 = ((bf16[8,2,12288]{2,1,0:T(2,128)(2,1)}), bf16[8,2,12288]{2,1,0:T(2,128)(2,1)}, u32[]{:S(2)}, u32[]{:S(2)}) async-start(bf16[8,2,12288]{2,1,0:T(2,128)(2,1)} %reshape.179), calls=%async_computation.2 | async-start | bytes 786432 | tf_op jit(solution)/shard_map/all_to_all | solution.py:30
  149.3 72.5 %all-gather.5.cloned.1.call-start = ((), (), s32[]{:S(2)}) async-start(), calls=%async_computation.8 | async-start | bytes 1966080 | tf_op jit(solution)/shard_map/all_gather | solution.py:24
  161.0 2.0 copy-start.3
  161.0 2.0 copy-start.5
  163.0 2.2 copy-start.1
  163.0 2.3 copy-start.20
  163.0 2.2 copy-start.22
  163.1 2.2 copy-start.25
  163.1 3.0 copy-start.26
  186.6 102.5 %reduce-scatter.5.cloned.1.call-start = ((), (), s32[]{:S(2)}) async-start(), calls=%async_computation.9 | async-start | bytes 3932160 | tf_op jit(solution)/shard_map/reduce_scatter | solution.py:29
  221.8 2.8 copy-start.2
  224.6 1.3 copy-start.14
  224.6 1.3 copy-start.16
  224.7 2.0 copy-start.7
  229.6 0.6 copy-start.24
  229.6 0.7 copy-start.19
  229.6 0.8 copy-start.21
  229.6 0.8 copy-start.23
  231.2 3.8 %copy-start.11 = (bf16[1,1,192,4096]{3,2,1,0:T(8,128)(2,1)S(1)}, bf16[1,1,192,4096]{3,2,1,0:T(8,128)(2,1)}, u32[]{:S(2)}) copy-start(bf16[1,1,192,4096]{3,2,1,0:T(8,128)(2,1)} %all-gather.3.cloned.1.call-done) | copy-start | bytes 4718596
  231.2 3.8 %copy-start.15 = (bf16[192,384]{1,0:T(8,128)(2,1)S(1)}, bf16[192,384]{1,0:T(8,128)(2,1)}, u32[]{:S(2)}) copy-start(bf16[192,384]{1,0:T(8,128)(2,1)} %copy-done.14) | copy-start | bytes 442372
  297.1 12.0 %all-to-all-start.3 = ((bf16[8,2,12288]{2,1,0:T(2,128)(2,1)}), bf16[8,2,12288]{2,1,0:T(2,128)(2,1)S(1)}, u32[]{:S(2)}, u32[]{:S(2)}) async-start(bf16[8,2,12288]{2,1,0:T(2,128)(2,1)} %reshape.181), calls=%async_computation.5 | async-start | bytes 786432 | tf_op jit(solution)/shard_map/all_to_all | solution.py:30
  300.8 4.3 %copy-start.12 = (bf16[1,1,192,4096]{3,2,1,0:T(8,128)(2,1)S(1)}, bf16[1,1,192,4096]{3,2,1,0:T(8,128)(2,1)}, u32[]{:S(2)}) copy-start(bf16[1,1,192,4096]{3,2,1,0:T(8,128)(2,1)} %all-gather.3.cloned.1.call-done) | copy-start | bytes 4718596
  300.8 4.3 %copy-start.17 = (bf16[192,384]{1,0:T(8,128)(2,1)S(1)}, bf16[192,384]{1,0:T(8,128)(2,1)}, u32[]{:S(2)}) copy-start(bf16[192,384]{1,0:T(8,128)(2,1)} %copy-done.16) | copy-start | bytes 442372
  310.2 1.9 copy-start.8
Sparse Core Ops, SparseCore 0:
  29.8 36.6 all-gather.2
  75.4 59.2 reduce-scatter.2
  186.7 35.0 all-gather.4
  229.7 59.2 reduce-scatter.4
where the time goes:
time: 321 us; the launch traced here: 320 us
  waiting for transfers between devices  189 us (59%)
  matrix products  36.2 us (11%)
  blocking collectives  28.8 us (9%)
  other arithmetic  22.5 us (7%)
  local copies, waits for them, and re-layouts  21.8 us (7%)
  between operations  14.1 us (4%)
  starting transfers between devices  8.09 us (3%)
    reduce_scatter x2, waiting for transfers between devices, collect(): lax.psum_scatter(partial_sums[None], 'local', scatter_dimension=2, tiled=...  109 us
    all_gather x2, waiting for transfers between devices, spread(): arrived = lax.all_gather(arrived, 'local', axis=2, tiled=True)  71.8 us
    all_to_all x2, blocking collectives, spread(): lax.all_to_all(buffer, 'node', split_axis=0, concat_axis=2, tiled=True)  28.8 us
    unnamed x59, local copies, waits for them, and re-layouts  11.5 us
    unnamed x2, other arithmetic  8.97 us
    all_to_all x2, waiting for transfers between devices, collect(): lax.all_to_all(summed.astype(jnp.bfloat16), 'node', split_axis=2, concat_...  7.99 us
    all_to_all x2, starting transfers between devices, collect(): lax.all_to_all(summed.astype(jnp.bfloat16), 'node', split_axis=2, concat_...  7.75 us
  transfers between devices with their start and end apart: 6, of which 6 were waited for; matrix products, arithmetic and copies ran while one was open for 5% of the time, Pallas kernels for 0%

commit v1 on v0

--- a/solution.py
+++ b/solution.py
@@ -5,6 +5,27 @@
 
 GSIZE = 8
 CAP = 6
+
+
+def laid_out(blocks, dim):
+    dims = list(blocks.shape[1:])
+    dims[dim] *= blocks.shape[0]
+    return jnp.moveaxis(blocks, 0, dim).reshape(dims)
+
+
+def doubled(array, axis):
+    size, mine = (lax.axis_size(axis), lax.axis_index(axis))
+    parts, bit = (array[None], 1)
+    while bit < size:
+        other = lax.ppermute(parts, axis, [(i, i ^ bit) for i in range(size)])
+        low = mine & bit == 0
+        parts = jnp.concatenate([jnp.where(low, parts, other), jnp.where(low, other, parts)])
+        bit *= 2
+    return parts
+
+
+def gather_by_bits(x, axis, dim):
+    return laid_out(doubled(x, axis), dim)
 
 
 def gate_weights(logits, group_ids, chosen, inside):
@@ -21,7 +42,7 @@
 
 def spread(buffer):
     arrived = lax.all_to_all(buffer, "node", split_axis=0, concat_axis=2, tiled=True)
-    arrived = lax.all_gather(arrived, "local", axis=2, tiled=True)
+    arrived = gather_by_bits(arrived, "local", 2)
     return arrived[0]
 
 

time: 321 us -> 350 us (1.090)
  waiting for transfers between devices: 189 us -> 204 us
  starting transfers between devices: 8.09 us -> 16 us
  other arithmetic: 22.5 us -> 27.5 us
  local copies, waits for them, and re-layouts: 21.8 us -> 26 us
  matrix products: 36.2 us -> 32.1 us
    ppermute x0 -> x4, waiting for transfers between devices: none -> 84.9 us  [doubled(): other = lax.ppermute(parts, axis, [(i, i ^ bit) for i in range(size)])]
    all_gather x2 -> x0, waiting for transfers between devices: 71.8 us -> none  [spread(): arrived = lax.all_gather(arrived, 'local', axis=2, tiled=True)]
    ppermute x0 -> x4, starting transfers between devices: none -> 7.95 us  [doubled(): other = lax.ppermute(parts, axis, [(i, i ^ bit) for i in range(size)])]
    unnamed x59 -> x69, local copies, waits for them, and re-layouts: 11.5 us -> 16.5 us
    all_to_all x2 -> x0, local copies, waits for them, and re-layouts: 3.84 us -> none  [spread(): lax.all_to_all(buffer, 'node', split_axis=0, concat_axis=2, tiled=True)]
    select_n x0 -> x4, other arithmetic: none -> 3.66 us  [doubled(): jnp.where(low, parts, other)]
  transfers between devices with their start and end apart: 6 -> 8, of which waited for: 6 -> 8; matrix products, arithmetic and copies ran while one was open for 5% -> 5% of each run, Pallas kernels for 0% -> 0%
where the time goes in v1:
time: 350 us; the launch traced here: 349 us
  waiting for transfers between devices  204 us (58%)
  matrix products  32.1 us (9%)
  blocking collectives  28.9 us (8%)
  other arithmetic  27.5 us (8%)
  local copies, waits for them, and re-layouts  26 us (7%)
  starting transfers between devices  16 us (5%)
  between operations  14.5 us (4%)
    reduce_scatter x2, waiting for transfers between devices, collect(): lax.psum_scatter(partial_sums[None], 'local', scatter_dimension=2, tiled=...  111 us
    ppermute x4, waiting for transfers between devices, doubled(): other = lax.ppermute(parts, axis, [(i, i ^ bit) for i in range(size)])  84.9 us
    all_to_all x2, blocking collectives, spread(): lax.all_to_all(buffer, 'node', split_axis=0, concat_axis=2, tiled=True)  28.9 us
    unnamed x69, local copies, waits for them, and re-layouts  16.5 us
    unnamed x2, other arithmetic  8.94 us
    ppermute x4, starting transfers between devices, doubled(): other = lax.ppermute(parts, axis, [(i, i ^ bit) for i in range(size)])  7.95 us
    all_to_all x2, starting transfers between devices, collect(): lax.all_to_all(summed.astype(jnp.bfloat16), 'node', split_axis=2, concat_...  7.76 us
    all_to_all x2, waiting for transfers between devices, collect(): lax.all_to_all(summed.astype(jnp.bfloat16), 'node', split_axis=2, concat_...  7.73 us
  transfers between devices with their start and end apart: 8, of which 8 were waited for; matrix products, arithmetic and copies ran while one was open for 5% of the time, Pallas kernels for 0%

profile of v1, /device:TPU:0, one launch (start us, length us, event | category | flops | bytes accessed | tf_op | source)
XLA Modules:
  0.0 348.5 jit_solution(10138919710854186527)
XLA Ops:
  7.2 0.8 broadcast_compare_fusion
  8.0 0.8 broadcast_multiply_fusion
  8.8 0.7 broadcast_select_fusion.8
  9.9 1.6 fusion.45
  11.8 0.9 reshape.172
  12.7 15.0 %all_to_all.16 = bf16[8,1,6,4096]{3,2,1,0:T(8,128)(2,1)} all-to-all(bf16[8,1,6,4096]{3,2,1,0:T(8,128)(2,1)} %bitcast.89), channel_id=1, replica_groups=mesh['node'=8,'local'=4] {'node'}, dimensions={0} | all-to-all | bytes 786432 | tf_op jit(solution)/shard_map/all_to_all | solution.py:44
  27.7 1.2 broadcast_in_dim.95
  28.9 1.9 collective-permute-start
  30.8 8.7 %collective-permute-done = bf16[1,1,1,48,4096]{4,3,2,1,0:T(8,128)(2,1)} collective-permute-done((bf16[1,1,1,48,4096]{4,3,2,1,0:T(8,128)(2,1)S(1)}, bf16[1,1,1,48,4096]{4,3,2,1,0:T(8,128)(2,1)}, u32[]{:S(2)}, u32[]{:S(2)}) %collective-permute-start) | collective-permute-done | bytes 393248 | tf_op jit(solution)/shard_map/ppermute | solution.py:20
  39.5 1.2 broadcast_select_fusion.7
  40.7 0.7 copy-done.10
  41.4 0.9 pad_maximum_fusion.2
  42.4 2.8 collective-permute-start.1
  45.1 33.3 %collective-permute-done.1 = bf16[2,1,1,48,4096]{4,3,2,1,0:T(8,128)(2,1)} collective-permute-done((bf16[2,1,1,48,4096]{4,3,2,1,0:T(8,128)(2,1)}, bf16[2,1,1,48,4096]{4,3,2,1,0:T(8,128)(2,1)}, u32[]{:S(2)}, u32[]{:S(2)}) %collective-permute-start.1) | collective-permute-done | bytes 786464 | tf_op jit(solution)/shard_map/ppermute | solution.py:20
  78.4 1.3 broadcast_select_fusion.3
  80.0 2.3 copy-done.2
  82.3 1.0 fusion.15
  83.2 0.9 copy-done.12
  84.1 1.7 multiply_convert_fusion.2
  85.9 0.7 copy-done.17
  86.5 2.7 convolution_bitcast_fusion
  89.2 0.8 copy-done.15
  90.8 59.5 %reduce-scatter.3.cloned.1.call-done = f32[1,1,48,4096]{3,2,1,0:T(8,128)} async-done(((f32[1,1,192,4096]{3,2,1,0:T(8,128)}), f32[1,1,48,4096]{3,2,1,0:T(8,128)}) %reduce-scatter.3.cloned.1.call-update) | async-done | bytes 786448 | tf_op jit(solution)/shard_map/reduce_scatter | solution.py:50
  150.3 1.2 convert_element_type.66
  151.5 1.7 copy.64
  153.8 4.8 %reduce = bf16[48,4096]{1,0:T(8,128)(2,1)} reduce(bf16[48,1,1,4096]{3,2,1,0:T(2,128)(2,1)} %bitcast.83, bf16[]{:T(256)} %broadcast.90), dimensions={1,2}, to_apply=%bitcast.76.reduce_sub_computation | reduce | bytes 786434
  158.6 2.1 reshape.181
  160.7 4.1 %all-to-all-start.1 = ((bf16[8,2,12288]{2,1,0:T(2,128)(2,1)}), bf16[8,2,12288]{2,1,0:T(2,128)(2,1)}, u32[]{:S(2)}, u32[]{:S(2)}) async-start(bf16[8,2,12288]{2,1,0:T(2,128)(2,1)} %reshape.181), calls=%async_computation.2 | async-start | bytes 786432 | tf_op jit(solution)/shard_map/all_to_all | solution.py:51
  166.4 6.7 %all-to-all-done.1 = bf16[8,2,12288]{2,1,0:T(2,128)(2,1)} async-done(((bf16[8,2,12288]{2,1,0:T(2,128)(2,1)}), bf16[8,2,12288]{2,1,0:T(2,128)(2,1)}, u32[]{:S(2)}, u32[]{:S(2)}) %all-to-all-start.1) | async-done | bytes 393248 | tf_op jit(solution)/shard_map/all_to_all | solution.py:51
  173.2 3.4 reshape.182
  176.5 2.0 fusion.29
  178.6 2.2 fusion.19
  180.8 0.8 fusion.43
  181.6 1.2 add_multiply_fusion
  183.3 1.2 fusion.6
  184.4 1.9 reshape.178
  186.3 13.8 %all_to_all.17 = bf16[8,1,6,4096]{3,2,1,0:T(8,128)(2,1)} all-to-all(bf16[8,1,6,4096]{3,2,1,0:T(8,128)(2,1)} %bitcast.90), channel_id=1, replica_groups=mesh['node'=8,'local'=4] {'node'}, dimensions={0} | all-to-all | bytes 786432 | tf_op jit(solution)/shard_map/all_to_all | solution.py:44
  200.2 1.9 broadcast_in_dim.97
  202.1 0.9 collective-permute-start.2
  203.0 9.6 %collective-permute-done.2 = bf16[1,1,1,48,4096]{4,3,2,1,0:T(8,128)(2,1)S(1)} collective-permute-done((bf16[1,1,1,48,4096]{4,3,2,1,0:T(8,128)(2,1)}, bf16[1,1,1,48,4096]{4,3,2,1,0:T(8,128)(2,1)S(1)}, u32[]{:S(2)}, u32[]{:S(2)}) %collective-permute-start.2) | collective-permute-done | bytes 393248 | tf_op jit(solution)/shard_map/ppermute | solution.py:20
  212.6 1.1 broadcast_select_fusion.5
  213.8 2.4 collective-permute-start.3
  216.1 33.3 %collective-permute-done.3 = bf16[2,1,1,48,4096]{4,3,2,1,0:T(8,128)(2,1)S(1)} collective-permute-done((bf16[2,1,1,48,4096]{4,3,2,1,0:T(8,128)(2,1)S(1)}, bf16[2,1,1,48,4096]{4,3,2,1,0:T(8,128)(2,1)S(1)}, u32[]{:S(2)}, u32[]{:S(2)}) %collective-permute-start.3) | collective-permute-done | bytes 786464 | tf_op jit(solution)/shard_map/ppermute | solution.py:20
  249.7 0.8 copy-done.31
  250.5 1.2 multiply_convert_fusion
  251.8 0.6 copy-done.3
  252.4 1.2 fusion.13
  253.7 0.6 copy-done.13
  254.3 2.9 fusion
  258.0 0.8 fusion.40
  258.8 3.8 %add_convert_fusion = bf16[128,4096]{1,0:T(8,128)(2,1)} fusion(f32[128,4096]{1,0:T(8,128)} %copy-done.1, f32[128,4096]{1,0:T(8,128)} %get-tuple-element.32, f32[128]{0:T(128)S(1)} %get-tuple-element.27, f32[128]{0:T(128)S(1)} %get-tuple-element.26), kind=kLoop, calls=%fused_computation.33 | loop fusion | flops 2097152 | bytes 5243904 | tf_op jit(solution)/shard_map/convert_element_type | solution.py:123
  262.6 3.0 fusion.1
  265.5 51.3 %reduce-scatter.5.cloned.1.call-done = f32[1,1,48,4096]{3,2,1,0:T(8,128)} async-done(((f32[1,1,192,4096]{3,2,1,0:T(8,128)}), f32[1,1,48,4096]{3,2,1,0:T(8,128)}) %reduce-scatter.5.cloned.1.call-update) | async-done | bytes 786448 | tf_op jit(solution)/shard_map/reduce_scatter | solution.py:50
  316.9 1.2 convert_element_type.74
  318.1 1.7 copy.63
  319.8 4.1 %reduce.1 = bf16[48,4096]{1,0:T(8,128)(2,1)S(1)} reduce(bf16[48,1,1,4096]{3,2,1,0:T(2,128)(2,1)} %bitcast.84, bf16[]{:T(256)} %broadcast.90), dimensions={1,2}, to_apply=%bitcast.75.reduce_sub_computation | reduce | bytes 786434
  323.9 1.1 reshape.183
  325.0 3.7 %all-to-all-start.3 = ((bf16[8,2,12288]{2,1,0:T(2,128)(2,1)}), bf16[8,2,12288]{2,1,0:T(2,128)(2,1)S(1)}, u32[]{:S(2)}, u32[]{:S(2)}) async-start(bf16[8,2,12288]{2,1,0:T(2,128)(2,1)} %reshape.183), calls=%async_computation.5 | async-start | bytes 786432 | tf_op jit(solution)/shard_map/all_to_all | solution.py:51
  328.7 4.3 %fusion.3 = bf16[1,384,4096]{2,1,0:T(8,128)(2,1)} fusion(bf16[192,384]{1,0:T(8,128)(2,1)} %copy-done.17, bf16[192,4096]{1,0:T(8,128)(2,1)} %bitcast.82), kind=kOutput, calls=%fused_computation.7 | convolution fusion | flops 605552640 | bytes 4866048 | tf_op jit(solution)/shard_map/erf,erd->efd/dot_general | solution.py:114
  333.0 3.0 fusion.2
  335.9 1.0 all-to-all-done.3
  336.9 1.1 reshape.184
  338.1 1.9 fusion.27
  340.0 1.7 fusion.4
  (89 shorter events, 5.5 us)
Async XLA Ops:
  7.2 79.4 %copy-start = (bf16[1,384,4096]{2,1,0:T(8,128)(2,1)S(1)}, bf16[1,384,4096]{2,1,0:T(8,128)(2,1)}, u32[]{:S(2)}) copy-start(bf16[1,384,4096]{2,1,0:T(8,128)(2,1)} %param.15) | copy-start | bytes 9437188
  7.2 143.1 %reduce-scatter.3.cloned.1.call-start = ((), (), s32[]{:S(2)}) async-start(), calls=%async_computation.6 | async-start | bytes 3932160 | tf_op jit(solution)/shard_map/reduce_scatter | solution.py:50
  9.8 1.7 copy-start.9
  28.9 2.0 copy-start.16
  28.9 10.6 %collective-permute-start = (bf16[1,1,1,48,4096]{4,3,2,1,0:T(8,128)(2,1)S(1)}, bf16[1,1,1,48,4096]{4,3,2,1,0:T(8,128)(2,1)}, u32[]{:S(2)}, u32[]{:S(2)}) collective-permute-start(bf16[1,1,1,48,4096]{4,3,2,1,0:T(8,128)(2,1)S(1)} %broadcast_in_dim.95), channel_id=1, source_target_pairs={{0,1},{1,0},{2,3},{3,2},{4,5},{5,4},{6,7},{7,6},{8,9},{9,8},{10,11... | collective-permute-start | bytes 1179656 | tf_op jit(solution)/shard_map/ppermute | solution.py:20
  40.7 0.7 copy-start.10
  42.4 36.1 %collective-permute-start.1 = (bf16[2,1,1,48,4096]{4,3,2,1,0:T(8,128)(2,1)}, bf16[2,1,1,48,4096]{4,3,2,1,0:T(8,128)(2,1)}, u32[]{:S(2)}, u32[]{:S(2)}) collective-permute-start(bf16[2,1,1,48,4096]{4,3,2,1,0:T(8,128)(2,1)} %pad_maximum_fusion.2), channel_id=1, source_target_pairs={{0,2},{1,3},{2,0},{3,1},{4,6},{5,7},{6,4},{7,5},{8,10},{9,11},{10,... | collective-permute-start | bytes 2359304 | tf_op jit(solution)/shard_map/ppermute | solution.py:20
  79.8 2.5 copy-start.2
  79.9 3.3 copy-start.5
  82.2 1.9 copy-start.12
  85.9 0.7 copy-start.17
  89.2 0.8 copy-start.15
  90.3 90.5 %copy-start.22 = (f32[128]{0:T(128)}, f32[128]{0:T(128)S(1)}, u32[]{:S(2)}) copy-start(f32[128]{0:T(128)S(1)} %fusion.54) | copy-start | bytes 1540
  160.7 12.4 %all-to-all-start.1 = ((bf16[8,2,12288]{2,1,0:T(2,128)(2,1)}), bf16[8,2,12288]{2,1,0:T(2,128)(2,1)}, u32[]{:S(2)}, u32[]{:S(2)}) async-start(bf16[8,2,12288]{2,1,0:T(2,128)(2,1)} %reshape.181), calls=%async_computation.2 | async-start | bytes 786432 | tf_op jit(solution)/shard_map/all_to_all | solution.py:51
  164.8 152.1 %reduce-scatter.5.cloned.1.call-start = ((), (), s32[]{:S(2)}) async-start(), calls=%async_computation.7 | async-start | bytes 3932160 | tf_op jit(solution)/shard_map/reduce_scatter | solution.py:50
  176.5 2.0 copy-start.4
  176.5 2.0 copy-start.11
  178.5 2.2 copy-start.1
  178.6 2.3 copy-start.24
  178.6 2.2 copy-start.26
  178.6 2.2 copy-start.29
  178.6 3.0 copy-start.30
  202.1 10.5 %collective-permute-start.2 = (bf16[1,1,1,48,4096]{4,3,2,1,0:T(8,128)(2,1)}, bf16[1,1,1,48,4096]{4,3,2,1,0:T(8,128)(2,1)S(1)}, u32[]{:S(2)}, u32[]{:S(2)}) collective-permute-start(bf16[1,1,1,48,4096]{4,3,2,1,0:T(8,128)(2,1)} %broadcast_in_dim.97), channel_id=1, source_target_pairs={{0,1},{1,0},{2,3},{3,2},{4,5},{5,4},{6,7},{7,6},{8,9},{9,8},{10,11... | collective-permute-start | bytes 1179656 | tf_op jit(solution)/shard_map/ppermute | solution.py:20
  213.8 35.7 %collective-permute-start.3 = (bf16[2,1,1,48,4096]{4,3,2,1,0:T(8,128)(2,1)S(1)}, bf16[2,1,1,48,4096]{4,3,2,1,0:T(8,128)(2,1)S(1)}, u32[]{:S(2)}, u32[]{:S(2)}) collective-permute-start(bf16[2,1,1,48,4096]{4,3,2,1,0:T(8,128)(2,1)S(1)} %pad_maximum_fusion.3), channel_id=1, source_target_pairs={{0,2},{1,3},{2,0},{3,1},{4,6},{5,7},{6,4},{7,5},{8,10},{9,11},{10,... | collective-permute-start | bytes 2359304 | tf_op jit(solution)/shard_map/ppermute | solution.py:20
  249.5 1.0 copy-start.31
  249.7 2.0 copy-start.8
  250.5 1.9 copy-start.3
  251.8 1.9 copy-start.18
  251.8 1.9 copy-start.20
  252.4 1.9 copy-start.13
  257.2 0.6 copy-start.28
  257.2 0.7 copy-start.23
  257.2 0.8 copy-start.25
  257.2 0.8 copy-start.27
  258.8 3.8 %copy-start.6 = (bf16[4,1,1,48,4096]{4,3,2,1,0:T(8,128)(2,1)S(1)}, bf16[4,1,1,48,4096]{4,3,2,1,0:T(8,128)(2,1)}, u32[]{:S(2)}) copy-start(bf16[4,1,1,48,4096]{4,3,2,1,0:T(8,128)(2,1)} %copy-done.5) | copy-start | bytes 4718596
  258.8 3.8 %copy-start.19 = (bf16[192,384]{1,0:T(8,128)(2,1)S(1)}, bf16[192,384]{1,0:T(8,128)(2,1)}, u32[]{:S(2)}) copy-start(bf16[192,384]{1,0:T(8,128)(2,1)} %copy-done.18) | copy-start | bytes 442372
  325.0 12.0 %all-to-all-start.3 = ((bf16[8,2,12288]{2,1,0:T(2,128)(2,1)}), bf16[8,2,12288]{2,1,0:T(2,128)(2,1)S(1)}, u32[]{:S(2)}, u32[]{:S(2)}) async-start(bf16[8,2,12288]{2,1,0:T(2,128)(2,1)} %reshape.183), calls=%async_computation.5 | async-start | bytes 786432 | tf_op jit(solution)/shard_map/all_to_all | solution.py:51
  328.7 4.3 %copy-start.7 = (bf16[4,1,1,48,4096]{4,3,2,1,0:T(8,128)(2,1)S(1)}, bf16[4,1,1,48,4096]{4,3,2,1,0:T(8,128)(2,1)}, u32[]{:S(2)}) copy-start(bf16[4,1,1,48,4096]{4,3,2,1,0:T(8,128)(2,1)} %copy-done.5) | copy-start | bytes 4718596
  328.7 4.3 %copy-start.21 = (bf16[192,384]{1,0:T(8,128)(2,1)S(1)}, bf16[192,384]{1,0:T(8,128)(2,1)}, u32[]{:S(2)}) copy-start(bf16[192,384]{1,0:T(8,128)(2,1)} %copy-done.20) | copy-start | bytes 442372
  338.1 1.9 copy-start.14
Sparse Core Ops, SparseCore 0:
  89.4 60.9 reduce-scatter.2
  257.4 59.4 reduce-scatter.4
